TPU v7x, 32 devices: a whole 2x2x4 slice. The times are simulated.
32 devices in a mesh: groups: 2 (over y), section: 8 (over z, x), sub: 2 (over core).
Axes of the slice: x: 2, y: 2, z: 4, core: 2. Of those that a mesh axis runs over, the one named last changes fastest.
Arguments:
- echoes: float32 [4, 384, 32, 256], P('groups', None, 'section', 'sub'), parts along dimension 0, may hold values from -6 to 6
- range_taps: float32 [2, 5], replicated, may hold values from -3 to 3
- pulse_taper: float32 [256], replicated, may hold values from 0.3 to 1
- channel_phase: float32 [256], replicated, may hold values from -3.140625 to 3.140625
- loading: float32 [1], replicated, may hold values from 0.5 to 2
- beam_index: int32 [256], replicated, may hold values from 0 to 1023
Outputs:
- normalized_beams: float32 [2, 256, 32, 256], P('groups', ('section', 'sub')), parts along dimension 0
There are 2 independent parts, one for each index of `groups`. A program takes and returns all parts, laid end to end along the dimension named above; an argument that names none is the same for every part. Nothing has to cross between parts.
All inputs are finite; a program needn't handle non-finite values. Where the computation divides by a largest or mean magnitude, that divisor is 1e-20 or more.
Results may differ from a plain program's by a relative error of at most 0.0003.
Values sent between devices are 32-bit elements; how exact they have to be, the bound alone decides.
A program may use at most 64 MiB of HBM per device.

v0:
```python
import functools
import math

import jax
import jax.numpy as jnp
import numpy as np
from jax import lax
from jax.experimental import pallas as pl
from jax.experimental.pallas import tpu as pltpu
from jax.sharding import PartitionSpec as P

PULSES = 256
INTERVALS = 2
ITERS = 2
LOOKS = 1024
HOP = 128


precise = lax.Precision.HIGHEST
epsilon = 1e-06


def apply_taps(pad_real, pad_imag, range_taps, gate_count):
    axis_gates = pad_real.ndim - 2
    shape_out = pad_real.shape[:axis_gates] + (gate_count,) + pad_real.shape[axis_gates + 1 :]
    out_real = jnp.zeros(shape_out, jnp.float32)
    out_imag = jnp.zeros(shape_out, jnp.float32)
    for offset in range(range_taps.shape[1]):
        part_real = lax.slice_in_dim(pad_real, offset, offset + gate_count, axis=axis_gates)
        part_imag = lax.slice_in_dim(pad_imag, offset, offset + gate_count, axis=axis_gates)
        out_real = out_real + range_taps[0, offset] * part_real - range_taps[1, offset] * part_imag
        out_imag = out_imag + range_taps[0, offset] * part_imag + range_taps[1, offset] * part_real
    return (out_real, out_imag)


def doppler_table(pulse_taper):
    pulse_count = pulse_taper.shape[0]
    pulse_index = jnp.arange(pulse_count, dtype=jnp.int32)
    product = pulse_index[:, None] * pulse_index[None, :] % pulse_count
    phase_angle = 2.0 * math.pi / pulse_count * product.astype(jnp.float32)
    cosine = jnp.cos(phase_angle) * pulse_taper[None, :]
    sine_part = jnp.sin(phase_angle) * pulse_taper[None, :]
    upper_rows = jnp.concatenate([cosine, sine_part], axis=1)
    lower_rows = jnp.concatenate([-sine_part, cosine], axis=1)
    return jnp.concatenate([upper_rows, lower_rows], axis=0)


def transform(doppler, segment):
    shape_in = segment.shape
    flattened = segment.reshape(shape_in[0] * shape_in[1], -1)
    result = jnp.dot(doppler, flattened, precision=precise, preferred_element_type=jnp.float32)
    return result.reshape(shape_in)


def batched(first, second):
    return jnp.einsum("dij,djk->dik", first, second, precision=precise)


def complex_product(left_real, left_imag, right_real, right_imag):
    out_real = batched(left_real, right_real) - batched(left_imag, right_imag)
    out_imag = batched(left_real, right_imag) + batched(left_imag, right_real)
    return (out_real, out_imag)


def gram_product(first, second):
    return jnp.einsum("dgi,dgj->dij", first, second, precision=precise)


def loaded_inverse(real_part, imag_part, loading):
    gate_count = real_part.shape[1]
    channels = real_part.shape[2]
    cov_real = (
        gram_product(real_part, real_part) + gram_product(imag_part, imag_part)
    ) / gate_count
    cov_imag = (
        gram_product(real_part, imag_part) - gram_product(imag_part, real_part)
    ) / gate_count
    identity = jnp.eye(channels, dtype=jnp.float32)
    trace_sum = jnp.sum(cov_real * identity[None], axis=(1, 2))
    cov_real = cov_real + (loading[0] * trace_sum / channels)[:, None, None] * identity[None]
    row_bound = jnp.max(jnp.sum(jnp.abs(cov_real) + jnp.abs(cov_imag), axis=2), axis=1)
    inv_real = identity[None] / row_bound[:, None, None]
    inv_imag = jnp.zeros_like(inv_real)
    for newton_step in range(ITERS):
        prod_real, prod_imag = complex_product(cov_real, cov_imag, inv_real, inv_imag)
        inv_real, inv_imag = complex_product(
            inv_real, inv_imag, 2.0 * identity[None] - prod_real, -prod_imag
        )
    return (inv_real, inv_imag)


def steering(beam_index, channel_phase):
    channels = channel_phase.shape[0]
    direction = -1.0 + (2.0 * beam_index.astype(jnp.float32) + 1.0) / LOOKS
    phase_angle = (
        math.pi * jnp.arange(channels, dtype=jnp.float32)[:, None] * direction[None, :]
        + channel_phase[:, None]
    )
    return (jnp.cos(phase_angle), jnp.sin(phase_angle))


def beam_weights(inv_real, inv_imag, steer_real, steer_imag):
    weight_real = jnp.einsum("dij,jb->dib", inv_real, steer_real, precision=precise) - jnp.einsum(
        "dij,jb->dib", inv_imag, steer_imag, precision=precise
    )
    weight_imag = jnp.einsum("dij,jb->dib", inv_real, steer_imag, precision=precise) + jnp.einsum(
        "dij,jb->dib", inv_imag, steer_real, precision=precise
    )
    gain_norm = jnp.sum(steer_real[None] * weight_real + steer_imag[None] * weight_imag, axis=1)
    return (weight_real / gain_norm[:, None, :], weight_imag / gain_norm[:, None, :])


def form_beams(data_real, data_imag, weight_real, weight_imag):
    out_real = jnp.einsum("dgc,dcb->dgb", data_real, weight_real, precision=precise) + jnp.einsum(
        "dgc,dcb->dgb", data_imag, weight_imag, precision=precise
    )
    out_imag = jnp.einsum("dgc,dcb->dgb", data_imag, weight_real, precision=precise) - jnp.einsum(
        "dgc,dcb->dgb", data_real, weight_imag, precision=precise
    )
    return out_real * out_real + out_imag * out_imag


def on_device(echoes, range_taps, pulse_taper, channel_phase, loading, beam_index):
    rim_width = range_taps.shape[1] // 2
    doppler = doppler_table(pulse_taper)
    spectra = [
        transform(
            doppler, lax.slice_in_dim(echoes, interval * HOP, interval * HOP + PULSES, axis=1)
        )
        for interval in range(INTERVALS)
    ]
    turned = [
        lax.all_to_all(
            lax.all_to_all(spectrum, "section", split_axis=1, concat_axis=2, tiled=True),
            "sub",
            split_axis=1,
            concat_axis=3,
            tiled=True,
        )
        for spectrum in spectra
    ]
    refined = []
    for spectrum in turned:
        padded_bins = jnp.pad(spectrum, ((0, 0), (0, 0), (rim_width, rim_width), (0, 0)))
        part_real, part_imag = apply_taps(
            padded_bins[0], padded_bins[1], range_taps, spectrum.shape[2]
        )
        refined.append(jnp.stack([part_real, part_imag]))
    turned = refined
    steer_real, steer_imag = steering(beam_index, channel_phase)
    interval = 0
    inv_real, inv_imag = loaded_inverse(turned[interval][0], turned[interval][1], loading)
    weight_real, weight_imag = beam_weights(inv_real, inv_imag, steer_real, steer_imag)
    beam_power = form_beams(
        turned[interval + 1][0], turned[interval + 1][1], weight_real, weight_imag
    )
    partials = [jnp.sum(beam_power, axis=(0, 1))]
    totals = lax.psum(jnp.stack(partials), ("section", "sub"))
    noise_level = totals / (PULSES * turned[0].shape[2])
    return jnp.stack([beam_power / (noise_level[0] + epsilon)])


MESH = pl.DeviceIdType.MESH
bf16 = jnp.bfloat16
f32 = jnp.float32


def fourier_rows(parts):
    index = np.arange(PULSES)
    angle = 2.0 * np.pi / PULSES * (index[:, None] * index[None, :] % PULSES)
    cosine, sine = np.cos(angle), np.sin(angle)
    real_rows = np.concatenate([cosine, sine], axis=1)
    imag_rows = np.concatenate([-sine, cosine], axis=1)
    own = PULSES // parts
    rows = np.stack([real_rows.reshape(parts, own, -1), imag_rows.reshape(parts, own, -1)], axis=1)
    return rows.reshape(2 * PULSES, 2 * PULSES).astype(np.float32)


def split(value):
    high = value.astype(bf16)
    return high, (value - high.astype(f32)).astype(bf16)


def dot3(left_high, left_low, right_high, right_low):
    out = jnp.dot(left_high, right_high, preferred_element_type=f32)
    out = out + jnp.dot(left_high, right_low, preferred_element_type=f32)
    return out + jnp.dot(left_low, right_high, preferred_element_type=f32)


def exact(left, right, dims):
    return lax.dot_general(left, right, (dims, ((), ())), precision=precise, preferred_element_type=f32)


def turned_pair(stacked):
    half = stacked.shape[0] // 2
    return jnp.concatenate([-stacked[half:], stacked[:half]], axis=0)


def kernel(
    sections, subs, gates, channels, bins,
    x_ref, rows_ref, taper_ref, steer_r_ref, steer_i_ref, taps_ref, loading_ref,
    power_ref, total_ref,
    table_h, table_l, steer_h, steer_l, send, recv, filt, beams, inner, scale, sums, gathered,
    send_sem, recv_sem, own_sem, sum_send_sem, sum_recv_sem,
):
    parts = sections * subs
    local_gates = gates // sections
    local_channels = channels // subs
    train = x_ref.shape[0] // 2
    taps = taps_ref.shape[1]
    half = taps // 2
    section = lax.axis_index("section")
    sub = lax.axis_index("sub")
    me = section * subs + sub
    rows = 2 * bins

    def place(step):
        peer = lax.rem(me + step, parts)
        return peer, {"section": peer // subs, "sub": lax.rem(peer, subs)}

    barrier = pltpu.get_barrier_semaphore()
    for step in range(1, parts):
        pl.semaphore_signal(barrier, inc=1, device_id=place(step)[1], device_id_type=MESH)

    high, low = split(rows_ref[...] * taper_ref[...])
    table_h[...] = high
    table_l[...] = low

    def piece(interval, step):
        peer, where = place(step)
        return pltpu.make_async_remote_copy(
            src_ref=send.at[interval, pl.ds(pl.multiple_of(peer * rows, rows), rows)],
            dst_ref=recv.at[interval, me + subs],
            send_sem=send_sem.at[interval, step - 1],
            recv_sem=recv_sem.at[interval, step - 1],
            device_id=where,
            device_id_type=MESH,
        )

    def own_piece(interval):
        return pltpu.make_async_copy(
            send.at[interval, pl.ds(pl.multiple_of(me * rows, rows), rows)],
            recv.at[interval, me + subs],
            own_sem.at[interval],
        )

    for interval in range(INTERVALS):
        start = interval * HOP
        segment = jnp.concatenate(
            [x_ref[start : start + PULSES], x_ref[train + start : train + start + PULSES]], axis=0
        )
        high, low = split(segment)
        send[interval] = dot3(table_h[...], table_l[...], high, low)
        if interval == 0:
            pl.semaphore_wait(barrier, parts - 1)
        own_piece(interval).start()
        for step in range(1, parts):
            piece(interval, step).start()

    for interval in range(INTERVALS):
        for slot in range(subs):
            recv[interval, slot] = jnp.zeros(recv.shape[2:], f32)
            recv[interval, subs + parts + slot] = jnp.zeros(recv.shape[2:], f32)

    steer_r, steer_i = steer_r_ref[...], steer_i_ref[...]
    steer_both = jnp.concatenate(
        [
            jnp.concatenate([steer_r, steer_i], axis=1),
            jnp.concatenate([-steer_i, steer_r], axis=1),
        ],
        axis=0,
    )
    high, low = split(steer_both)
    steer_h[...] = high
    steer_l[...] = low

    def refine(interval, sign):
        own_piece(interval).wait()
        for step in range(1, parts):
            piece(interval, step).wait()

        def one(slot, carry):
            here = slot // subs
            columns = lax.rem(slot, subs)

            def gate(offset):
                shift = offset // local_gates
                column = (offset % local_gates) * local_channels
                block = recv[interval, slot + subs * (1 + shift), :, column : column + local_channels]
                return block[:bins], block[bins:]

            around = {offset: gate(offset) for offset in range(-half, local_gates + half)}
            for local in range(local_gates):
                real = jnp.zeros((bins, local_channels), f32)
                imag = jnp.zeros((bins, local_channels), f32)
                for tap in range(taps):
                    part_r, part_i = around[local + tap - half]
                    tap_r, tap_i = taps_ref[0, tap], taps_ref[1, tap]
                    real = real + tap_r * part_r - tap_i * part_i
                    imag = imag + tap_r * part_i + tap_i * part_r
                row = pl.multiple_of((here * local_gates + local) * bins, bins)
                filt[interval, columns, pl.ds(row, bins)] = real
                filt[interval, columns, pl.ds(row + gates * bins, bins)] = sign * imag
            return carry

        lax.fori_loop(0, parts, one, 0)
        count = gates * bins
        both = jnp.concatenate(
            [filt[interval, block, start : start + count] for start in (0, count) for block in range(subs)],
            axis=1,
        )
        high, low = split(both)
        out = dot3(high, low, steer_h[...], steer_l[...])
        lanes = beams.shape[2]
        blocks = beams.shape[0]
        for block in range(2 * blocks):
            start = block // blocks * count
            beams[block % blocks, start : start + count] = out[:, block * lanes : (block + 1) * lanes]

    def rows_of(ref, index):
        return jnp.concatenate(
            [ref[block, pl.ds(index, 2 * gates, stride=bins), :] for block in range(ref.shape[0])], axis=1
        )

    def solve(index, carry):
        data = rows_of(filt.at[0], index)
        aside = turned_pair(data)
        trace = jnp.sum(jnp.sum(data * data, axis=0, keepdims=True), axis=1, keepdims=True) / gates
        loaded = loading_ref[0] * trace / channels
        data_h, data_l = split(data)
        aside_h, aside_l = split(aside)
        left = jnp.concatenate([data_h, data_l, data_h, data_l], axis=0)
        right_r = jnp.concatenate([data_h, data_h, data_l, data_l], axis=0)
        right_i = jnp.concatenate([aside_h, aside_h, aside_l, aside_l], axis=0)
        dims = (((0,), (0,)), ((), ()))
        cov_r = lax.dot_general(left, right_r, dims, preferred_element_type=f32)
        cov_i = lax.dot_general(left, right_i, dims, preferred_element_type=f32)
        sums_of = jnp.sum(jnp.abs(cov_r) + jnp.abs(cov_i), axis=0, keepdims=True)
        bound = jnp.max(sums_of, axis=1, keepdims=True) / gates + loaded
        unit = 1.0 / (gates * bound)
        shift = loaded / bound
        across = ((1,), (1,))
        gram = (exact(data, data, across) + exact(aside, aside, across)) * unit
        square = exact(gram, gram, ((1,), (0,)))
        row_index = lax.broadcasted_iota(jnp.int32, gram.shape, 0)
        column_index = lax.broadcasted_iota(jnp.int32, gram.shape, 1)
        zeroth = jnp.where(row_index == column_index, -6.0 + 8.0 * shift - 3.0 * shift * shift, 0.0)
        poly = zeroth + (4.0 - 3.0 * shift) * gram - square
        plain = 4.0 - 6.0 * shift + 4.0 * shift * shift - shift * shift * shift
        toward = rows_of(beams, index)
        moved = exact(poly, toward, ((1,), (0,)))
        gain = plain * channels + unit * jnp.sum(toward * moved, axis=0, keepdims=True)
        inner[index] = moved * (unit / gain)
        scale[index] = plain / gain
        return carry

    def form(index, carry):
        data = rows_of(filt.at[0], index)
        later = rows_of(filt.at[1], index)
        across = ((1,), (1,))
        cross = exact(later, data, across) + exact(turned_pair(later), turned_pair(data), across)
        out = rows_of(beams, index) * scale[index] + exact(cross, inner[index], ((1,), (0,)))
        power = out[:gates] * out[:gates] + out[gates:] * out[gates:]
        power_ref[index] = power
        return carry + jnp.sum(power.reshape(gates // 8, 8, -1), axis=0)

    refine(0, 1.0)
    lax.fori_loop(0, bins, solve, 0)
    refine(1, -1.0)
    sums[...] = lax.fori_loop(0, bins, form, jnp.zeros(sums.shape, f32))

    def sum_piece(step):
        return pltpu.make_async_remote_copy(
            src_ref=sums,
            dst_ref=gathered.at[step - 1],
            send_sem=sum_send_sem.at[step - 1],
            recv_sem=sum_recv_sem.at[step - 1],
            device_id=place(step)[1],
            device_id_type=MESH,
        )

    for step in range(1, parts):
        sum_piece(step).start()
    total = sums[...]
    for step in range(1, parts):
        sum_piece(step).wait()
    for step in range(1, parts):
        total = total + gathered[step - 1]
    total_ref[...] = total


def fused(sections, subs, echoes, range_taps, pulse_taper, channel_phase, loading, beam_index):
    parts = sections * subs
    local_gates, local_channels = echoes.shape[2:]
    gates, channels = local_gates * sections, local_channels * subs
    bins = PULSES // parts
    beam_count = beam_index.shape[0]
    flat = echoes.reshape(2 * echoes.shape[1], local_gates * local_channels)
    steer_real, steer_imag = steering(beam_index, channel_phase)
    taper = jnp.concatenate([pulse_taper, pulse_taper])[None, :]
    vmem = pl.BlockSpec(memory_space=pltpu.VMEM)
    smem = pl.BlockSpec(memory_space=pltpu.SMEM)
    power, total = pl.pallas_call(
        functools.partial(kernel, sections, subs, gates, channels, bins),
        out_shape=(
            jax.ShapeDtypeStruct((bins, gates, beam_count), f32),
            jax.ShapeDtypeStruct((8, beam_count), f32),
        ),
        in_specs=[vmem] * 5 + [smem] * 2,
        out_specs=(vmem, vmem),
        scratch_shapes=[
            pltpu.VMEM((2 * PULSES, 2 * PULSES), bf16),
            pltpu.VMEM((2 * PULSES, 2 * PULSES), bf16),
            pltpu.VMEM((2 * channels, 2 * beam_count), bf16),
            pltpu.VMEM((2 * channels, 2 * beam_count), bf16),
            pltpu.VMEM((INTERVALS, 2 * PULSES, local_gates * local_channels), f32),
            pltpu.VMEM((INTERVALS, parts + 2 * subs, 2 * bins, local_gates * local_channels), f32),
            pltpu.VMEM((INTERVALS, subs, 2 * gates * bins, local_channels), f32),
            pltpu.VMEM((beam_count // 128, 2 * gates * bins, 128), f32),
            pltpu.VMEM((bins, 2 * gates, beam_count), f32),
            pltpu.VMEM((bins, 1, beam_count), f32),
            pltpu.VMEM((8, beam_count), f32),
            pltpu.VMEM((parts - 1, 8, beam_count), f32),
            pltpu.SemaphoreType.DMA((INTERVALS, parts - 1)),
            pltpu.SemaphoreType.DMA((INTERVALS, parts - 1)),
            pltpu.SemaphoreType.DMA((INTERVALS,)),
            pltpu.SemaphoreType.DMA((parts - 1,)),
            pltpu.SemaphoreType.DMA((parts - 1,)),
        ],
        compiler_params=pltpu.CompilerParams(
            collective_id=0, has_side_effects=True, vmem_limit_bytes=56 * 2**20
        ),
        name="beams",
    )(flat, jnp.asarray(fourier_rows(parts)), taper, steer_real, steer_imag, range_taps, loading)
    noise_level = jnp.sum(total, axis=0) / (PULSES * gates)
    return (power / (noise_level + epsilon))[None]


def solution(mesh):
    sections, subs = mesh.shape["section"], mesh.shape["sub"]
    parts = sections * subs

    def body(echoes, *rest):
        local_gates, local_channels = echoes.shape[2:]
        gates, channels = local_gates * sections, local_channels * subs
        fits = (
            PULSES % parts == 0
            and (PULSES // parts) % 8 == 0
            and gates % 8 == 0
            and 2 * gates <= channels
            and local_channels == 128
            and rest[-1].shape[0] % 128 == 0
            and local_gates >= rest[0].shape[1] // 2
            and channels == rest[-1].shape[0]
        )
        if fits:
            return fused(sections, subs, echoes, *rest)
        return on_device(echoes, *rest)

    in_specs = (P("groups", None, "section", "sub"), P(), P(), P(), P(), P())
    out_specs = P("groups", ("section", "sub"), None, None)
    return jax.shard_map(
        body, mesh=mesh, in_specs=in_specs, out_specs=out_specs, check_vma=False
    )
```

profile of v0, /device:TPU:0, one launch (start us, length us, event | category | flops | bytes accessed | tf_op | source)
XLA Modules:
  0.0 84.1 jit_solution(10769649471406079503)
XLA Ops:
  0.7 1.4 %pad_maximum_fusion = f32[512]{0:T(512)} fusion(f32[256]{0:T(256)} %param.9), kind=kLoop, calls=%fused_computation.5 | loop fusion | flops 512 | bytes 3072 | tf_op jit(solution)/shard_map/concatenate | solution.py:400
  2.0 0.7 multiply_add_fusion.2
  2.7 2.6 %fusion = (f32[256,256]{1,0:T(8,128)}, f32[256,256]{1,0:T(8,128)}) fusion(f32[256]{0:T(256)} %param.10, f32[256]{0:T(256)S(1)} %get-tuple-element.11, f32[256]{0:T(256)S(1)} %get-tuple-element.12), kind=kLoop, calls=%fused_computation.3 | loop fusion | flops 131072 | bytes 527360 | tf_op jit(solution)/shard_map/sin | solution.py:99
  5.3 2.7 %copy.10 = f32[96,8,4,128]{3,1,2,0:T(8,128)} copy(f32[96,8,4,128]{3,2,1,0:T(4,128)} %bitcast.9) | data formatting | bytes 3145728
  7.9 73.6 %beams.1 = (f32[16,32,256]{2,1,0:T(8,128)}, f32[8,256]{1,0:T(8,128)}) custom-call(f32[768,512]{1,0:T(8,128)} %bitcast.8, f32[512,512]{1,0:T(8,128)} %constant.20.clone.rows_ref, f32[1,512]{1,0:T(1,128)} %bitcast.10, f32[256,256]{1,0:T(8,128)} %get-tuple-element.10.steer_r_ref, f32[256,256]{1,0:T(8,128)} %get-tuple-element.9.steer_i_ref, f32[2,5]{1,0:T(2,128)} %taps_ref.1, ...), custom_call_target="tpu_custom_call" | custom-call | tf_op jit(solution)/shard_map/beams/pallas_call | solution.py:403
  81.5 0.7 reduce_sum.9
  82.3 1.9 %divide_bitcast_fusion = f32[1,16,32,256]{3,2,1,0:T(8,128)} fusion(f32[16,32,256]{2,1,0:T(8,128)} %get-tuple-element.7, f32[256]{0:T(256)S(1)} %multiply_add_fusion.1), kind=kLoop, calls=%fused_computation.1 | loop fusion | flops 131072 | bytes 1049600 | tf_op jit(solution)/shard_map/broadcast_in_dim | solution.py:436
  (1 shorter events, 0.0 us)
where the time goes:
time: 84.4 us; the launch traced here: 84.1 us
  Pallas kernels  73.6 us (87%)
  other arithmetic  7.21 us (9%)
  local copies, waits for them, and re-layouts  2.68 us (3%)
    pallas_call x1, Pallas kernels, fused(): pl.pallas_call(functools.partial(kernel, sections, subs, gates, channels,...  73.6 us
    unnamed x1, local copies, waits for them, and re-layouts  2.68 us
    sin x1, other arithmetic, steering(): return (jnp.cos(phase_angle), jnp.sin(phase_angle))  2.56 us
    broadcast_in_dim x1, other arithmetic, fused(): return (power / (noise_level + epsilon))[None]  1.89 us

commit v1 on v0

--- a/solution.py
+++ b/solution.py
@@ -163,6 +163,7 @@
 MESH = pl.DeviceIdType.MESH
 bf16 = jnp.bfloat16
 f32 = jnp.float32
+BLOCK = 8
 
 
 def fourier_rows(parts):
@@ -171,8 +172,8 @@
     cosine, sine = np.cos(angle), np.sin(angle)
     real_rows = np.concatenate([cosine, sine], axis=1)
     imag_rows = np.concatenate([-sine, cosine], axis=1)
-    own = PULSES // parts
-    rows = np.stack([real_rows.reshape(parts, own, -1), imag_rows.reshape(parts, own, -1)], axis=1)
+    split_rows = [part.reshape(parts, -1, BLOCK, 2 * PULSES) for part in (real_rows, imag_rows)]
+    rows = np.stack(split_rows, axis=2).transpose(1, 0, 2, 3, 4)
     return rows.reshape(2 * PULSES, 2 * PULSES).astype(np.float32)
 
 
@@ -187,6 +188,13 @@
     return out + jnp.dot(left_low, right_high, preferred_element_type=f32)
 
 
+def dot3_across(left_high, left_low, right_high, right_low):
+    dims = (((1,), (1,)), ((), ()))
+    out = lax.dot_general(left_high, right_high, dims, preferred_element_type=f32)
+    out = out + lax.dot_general(left_high, right_low, dims, preferred_element_type=f32)
+    return out + lax.dot_general(left_low, right_high, dims, preferred_element_type=f32)
+
+
 def exact(left, right, dims):
     return lax.dot_general(left, right, (dims, ((), ())), precision=precise, preferred_element_type=f32)
 
@@ -198,71 +206,112 @@
 
 def kernel(
     sections, subs, gates, channels, bins,
-    x_ref, rows_ref, taper_ref, steer_r_ref, steer_i_ref, taps_ref, loading_ref,
-    power_ref, total_ref,
-    table_h, table_l, steer_h, steer_l, send, recv, filt, beams, inner, scale, sums, gathered,
-    send_sem, recv_sem, own_sem, sum_send_sem, sum_recv_sem,
+    x_hbm, rows_hbm, taper_ref, phase_ref, beam_ref, taps_ref, loading_ref,
+    power_hbm, noise_ref,
+    x_ref, rows_ref, table_h, table_l, steer_h, steer_l, send, recv, filt, beams,
+    conj_h, conj_l, inner_h, inner_l, scale, power_ref, sums, gathered,
+    x_sem, rows_sem, send_sem, recv_sem, own_sem, sum_send_sem, sum_recv_sem, out_sem,
 ):
     parts = sections * subs
     local_gates = gates // sections
     local_channels = channels // subs
-    train = x_ref.shape[0] // 2
+    train = x_ref.shape[0] // (2 * local_gates)
     taps = taps_ref.shape[1]
     half = taps // 2
+    groups_of_bins = bins // BLOCK
     section = lax.axis_index("section")
     sub = lax.axis_index("sub")
     me = section * subs + sub
-    rows = 2 * bins
+    rows = 2 * BLOCK
+    steps = list(range(parts - 1, 0, -1))
 
     def place(step):
-        peer = lax.rem(me + step, parts)
+        peer = me ^ step
         return peer, {"section": peer // subs, "sub": lax.rem(peer, subs)}
 
+    first = PULSES * local_gates
+    rest = (train - PULSES) * local_gates
+    x_copies = []
+    for number, (start, length) in enumerate(
+        [(0, first), (train * local_gates, first), (first, rest), (train * local_gates + first, rest)]
+    ):
+        x_copies.append(
+            pltpu.make_async_copy(
+                x_hbm.at[pl.ds(start, length)], x_ref.at[pl.ds(start, length)], x_sem.at[number]
+            )
+        )
+    rows_copy = pltpu.make_async_copy(rows_hbm, rows_ref, rows_sem)
+    rows_copy.start()
+    for copy in x_copies:
+        copy.start()
     barrier = pltpu.get_barrier_semaphore()
-    for step in range(1, parts):
+    for step in steps:
         pl.semaphore_signal(barrier, inc=1, device_id=place(step)[1], device_id_type=MESH)
 
-    high, low = split(rows_ref[...] * taper_ref[...])
+    taper = jnp.concatenate([taper_ref[...], taper_ref[...]], axis=1)
+    rows_copy.wait()
+    high, low = split(rows_ref[...] * taper)
     table_h[...] = high
     table_l[...] = low
 
-    def piece(interval, step):
+    def piece(unit, step):
         peer, where = place(step)
         return pltpu.make_async_remote_copy(
-            src_ref=send.at[interval, pl.ds(pl.multiple_of(peer * rows, rows), rows)],
-            dst_ref=recv.at[interval, me + subs],
-            send_sem=send_sem.at[interval, step - 1],
-            recv_sem=recv_sem.at[interval, step - 1],
+            src_ref=send.at[unit, pl.ds(pl.multiple_of(peer * rows, rows), rows)],
+            dst_ref=recv.at[unit, me + subs],
+            send_sem=send_sem.at[unit, step - 1],
+            recv_sem=recv_sem.at[unit, step - 1],
             device_id=where,
             device_id_type=MESH,
         )
 
-    def own_piece(interval):
+    def own_piece(unit):
         return pltpu.make_async_copy(
-            send.at[interval, pl.ds(pl.multiple_of(me * rows, rows), rows)],
-            recv.at[interval, me + subs],
-            own_sem.at[interval],
+            send.at[unit, pl.ds(pl.multiple_of(me * rows, rows), rows)],
+            recv.at[unit, me + subs],
+            own_sem.at[unit],
         )
 
     for interval in range(INTERVALS):
-        start = interval * HOP
+        x_copies[2 * interval].wait()
+        x_copies[2 * interval + 1].wait()
         segment = jnp.concatenate(
-            [x_ref[start : start + PULSES], x_ref[train + start : train + start + PULSES]], axis=0
+            [
+                jnp.concatenate(
+                    [
+                        x_ref[
+                            pl.ds((part * train + interval * HOP) * local_gates + gate, PULSES, stride=local_gates), :
+                        ]
+                        for gate in range(local_gates)
+                    ],
+                    axis=1,
+                )
+                for part in range(2)
+            ],
+            axis=0,
         )
         high, low = split(segment)
-        send[interval] = dot3(table_h[...], table_l[...], high, low)
-        if interval == 0:
-            pl.semaphore_wait(barrier, parts - 1)
-        own_piece(interval).start()
-        for step in range(1, parts):
-            piece(interval, step).start()
-
-    for interval in range(INTERVALS):
+        for group in range(groups_of_bins):
+            unit = interval * groups_of_bins + group
+            of_group = slice(group * parts * rows, (group + 1) * parts * rows)
+            send[unit] = dot3(table_h[of_group], table_l[of_group], high, low)
+            if unit == 0:
+                pl.semaphore_wait(barrier, parts - 1)
+            for step in steps:
+                piece(unit, step).start()
+            own_piece(unit).start()
+
+    for unit in range(recv.shape[0]):
         for slot in range(subs):
-            recv[interval, slot] = jnp.zeros(recv.shape[2:], f32)
-            recv[interval, subs + parts + slot] = jnp.zeros(recv.shape[2:], f32)
-
-    steer_r, steer_i = steer_r_ref[...], steer_i_ref[...]
+            recv[unit, slot] = jnp.zeros(recv.shape[2:], f32)
+            recv[unit, subs + parts + slot] = jnp.zeros(recv.shape[2:], f32)
+
+    direction = -1.0 + (2.0 * beam_ref[...].astype(f32) + 1.0) / LOOKS
+    beam_count = direction.shape[1]
+    channel = lax.broadcasted_iota(jnp.int32, (channels, beam_count), 0).astype(f32)
+    phase = jnp.transpose(jnp.broadcast_to(phase_ref[...], (beam_count, channels)))
+    angle = math.pi * channel * direction + phase
+    steer_r, steer_i = jnp.cos(angle), jnp.sin(angle)
     steer_both = jnp.concatenate(
         [
             jnp.concatenate([steer_r, steer_i], axis=1),
@@ -274,10 +323,10 @@
     steer_h[...] = high
     steer_l[...] = low
 
-    def refine(interval, sign):
-        own_piece(interval).wait()
-        for step in range(1, parts):
-            piece(interval, step).wait()
+    def refine(unit, sign):
+        own_piece(unit).wait()
+        for step in steps:
+            piece(unit, step).wait()
 
         def one(slot, carry):
             here = slot // subs
@@ -286,27 +335,27 @@
             def gate(offset):
                 shift = offset // local_gates
                 column = (offset % local_gates) * local_channels
-                block = recv[interval, slot + subs * (1 + shift), :, column : column + local_channels]
-                return block[:bins], block[bins:]
+                block = recv[unit, slot + subs * (1 + shift), :, column : column + local_channels]
+                return block[:BLOCK], block[BLOCK:]
 
             around = {offset: gate(offset) for offset in range(-half, local_gates + half)}
             for local in range(local_gates):
-                real = jnp.zeros((bins, local_channels), f32)
-                imag = jnp.zeros((bins, local_channels), f32)
+                real = jnp.zeros((BLOCK, local_channels), f32)
+                imag = jnp.zeros((BLOCK, local_channels), f32)
                 for tap in range(taps):
                     part_r, part_i = around[local + tap - half]
                     tap_r, tap_i = taps_ref[0, tap], taps_ref[1, tap]
                     real = real + tap_r * part_r - tap_i * part_i
                     imag = imag + tap_r * part_i + tap_i * part_r
-                row = pl.multiple_of((here * local_gates + local) * bins, bins)
-                filt[interval, columns, pl.ds(row, bins)] = real
-                filt[interval, columns, pl.ds(row + gates * bins, bins)] = sign * imag
+                row = pl.multiple_of((here * local_gates + local) * BLOCK, BLOCK)
+                filt[columns, pl.ds(row, BLOCK)] = real
+                filt[columns, pl.ds(row + gates * BLOCK, BLOCK)] = sign * imag
             return carry
 
-        lax.fori_loop(0, parts, one, 0)
-        count = gates * bins
+        lax.fori_loop(0, parts, one, 0, unroll=2)
+        count = gates * BLOCK
         both = jnp.concatenate(
-            [filt[interval, block, start : start + count] for start in (0, count) for block in range(subs)],
+            [filt[block, start : start + count] for start in (0, count) for block in range(subs)],
             axis=1,
         )
         high, low = split(both)
@@ -319,11 +368,11 @@
 
     def rows_of(ref, index):
         return jnp.concatenate(
-            [ref[block, pl.ds(index, 2 * gates, stride=bins), :] for block in range(ref.shape[0])], axis=1
-        )
-
-    def solve(index, carry):
-        data = rows_of(filt.at[0], index)
+            [ref[block, pl.ds(index, 2 * gates, stride=BLOCK), :] for block in range(ref.shape[0])], axis=1
+        )
+
+    def solve(group, index, carry):
+        data = rows_of(filt, index)
         aside = turned_pair(data)
         trace = jnp.sum(jnp.sum(data * data, axis=0, keepdims=True), axis=1, keepdims=True) / gates
         loaded = loading_ref[0] * trace / channels
@@ -339,8 +388,9 @@
         bound = jnp.max(sums_of, axis=1, keepdims=True) / gates + loaded
         unit = 1.0 / (gates * bound)
         shift = loaded / bound
-        across = ((1,), (1,))
-        gram = (exact(data, data, across) + exact(aside, aside, across)) * unit
+        full_h = jnp.concatenate([data_h, aside_h], axis=1)
+        full_l = jnp.concatenate([data_l, aside_l], axis=1)
+        gram = dot3_across(full_h, full_l, full_h, full_l) * unit
         square = exact(gram, gram, ((1,), (0,)))
         row_index = lax.broadcasted_iota(jnp.int32, gram.shape, 0)
         column_index = lax.broadcasted_iota(jnp.int32, gram.shape, 1)
@@ -350,24 +400,39 @@
         toward = rows_of(beams, index)
         moved = exact(poly, toward, ((1,), (0,)))
         gain = plain * channels + unit * jnp.sum(toward * moved, axis=0, keepdims=True)
-        inner[index] = moved * (unit / gain)
-        scale[index] = plain / gain
+        place_of = group * BLOCK + index
+        high, low = split(moved * (unit / gain))
+        inner_h[place_of] = high
+        inner_l[place_of] = low
+        conj_h[place_of] = full_h
+        conj_l[place_of] = full_l
+        scale[place_of] = plain / gain
         return carry
 
-    def form(index, carry):
-        data = rows_of(filt.at[0], index)
-        later = rows_of(filt.at[1], index)
-        across = ((1,), (1,))
-        cross = exact(later, data, across) + exact(turned_pair(later), turned_pair(data), across)
-        out = rows_of(beams, index) * scale[index] + exact(cross, inner[index], ((1,), (0,)))
+    def form(group, index, carry):
+        place_of = group * BLOCK + index
+        later = rows_of(filt, index)
+        high, low = split(jnp.concatenate([later, turned_pair(later)], axis=1))
+        cross = dot3_across(high, low, conj_h[place_of], conj_l[place_of])
+        high, low = split(cross)
+        out = rows_of(beams, index) * scale[place_of] + dot3(high, low, inner_h[place_of], inner_l[place_of])
         power = out[:gates] * out[:gates] + out[gates:] * out[gates:]
-        power_ref[index] = power
+        power_ref[place_of] = power
         return carry + jnp.sum(power.reshape(gates // 8, 8, -1), axis=0)
 
-    refine(0, 1.0)
-    lax.fori_loop(0, bins, solve, 0)
-    refine(1, -1.0)
-    sums[...] = lax.fori_loop(0, bins, form, jnp.zeros(sums.shape, f32))
+    for group in range(groups_of_bins):
+        refine(group, 1.0)
+        lax.fori_loop(0, BLOCK, functools.partial(solve, group), 0, unroll=2)
+    total = jnp.zeros(sums.shape, f32)
+    out_copies = []
+    for group in range(groups_of_bins):
+        refine(groups_of_bins + group, -1.0)
+        total = lax.fori_loop(0, BLOCK, functools.partial(form, group), total, unroll=4)
+        span = pl.ds(group * BLOCK, BLOCK)
+        out_copies.append(pltpu.make_async_copy(power_ref.at[span], power_hbm.at[span], out_sem.at[group]))
+        if group < groups_of_bins - 1:
+            out_copies[-1].start()
+    sums[...] = total
 
     def sum_piece(step):
         return pltpu.make_async_remote_copy(
@@ -379,14 +444,16 @@
             device_id_type=MESH,
         )
 
-    for step in range(1, parts):
+    for step in steps:
         sum_piece(step).start()
-    total = sums[...]
-    for step in range(1, parts):
+    out_copies[-1].start()
+    for step in steps:
         sum_piece(step).wait()
-    for step in range(1, parts):
+    for step in steps:
         total = total + gathered[step - 1]
-    total_ref[...] = total
+    noise_ref[...] = jnp.sum(total, axis=0, keepdims=True) / (PULSES * gates) + epsilon
+    for copy in out_copies:
+        copy.wait()
 
 
 def fused(sections, subs, echoes, range_taps, pulse_taper, channel_phase, loading, beam_index):
@@ -395,45 +462,57 @@
     gates, channels = local_gates * sections, local_channels * subs
     bins = PULSES // parts
     beam_count = beam_index.shape[0]
-    flat = echoes.reshape(2 * echoes.shape[1], local_gates * local_channels)
-    steer_real, steer_imag = steering(beam_index, channel_phase)
-    taper = jnp.concatenate([pulse_taper, pulse_taper])[None, :]
+    units = INTERVALS * bins // BLOCK
+    width = local_gates * local_channels
+    flat = echoes.reshape(2 * echoes.shape[1] * local_gates, local_channels)
     vmem = pl.BlockSpec(memory_space=pltpu.VMEM)
     smem = pl.BlockSpec(memory_space=pltpu.SMEM)
-    power, total = pl.pallas_call(
+    whole = pl.BlockSpec(memory_space=pl.ANY)
+    power, noise_level = pl.pallas_call(
         functools.partial(kernel, sections, subs, gates, channels, bins),
         out_shape=(
             jax.ShapeDtypeStruct((bins, gates, beam_count), f32),
-            jax.ShapeDtypeStruct((8, beam_count), f32),
+            jax.ShapeDtypeStruct((1, beam_count), f32),
         ),
-        in_specs=[vmem] * 5 + [smem] * 2,
-        out_specs=(vmem, vmem),
+        in_specs=[whole] * 2 + [vmem] * 3 + [smem] * 2,
+        out_specs=(whole, vmem),
         scratch_shapes=[
+            pltpu.VMEM(flat.shape, f32),
+            pltpu.VMEM((2 * PULSES, 2 * PULSES), f32),
             pltpu.VMEM((2 * PULSES, 2 * PULSES), bf16),
             pltpu.VMEM((2 * PULSES, 2 * PULSES), bf16),
             pltpu.VMEM((2 * channels, 2 * beam_count), bf16),
             pltpu.VMEM((2 * channels, 2 * beam_count), bf16),
-            pltpu.VMEM((INTERVALS, 2 * PULSES, local_gates * local_channels), f32),
-            pltpu.VMEM((INTERVALS, parts + 2 * subs, 2 * bins, local_gates * local_channels), f32),
-            pltpu.VMEM((INTERVALS, subs, 2 * gates * bins, local_channels), f32),
-            pltpu.VMEM((beam_count // 128, 2 * gates * bins, 128), f32),
-            pltpu.VMEM((bins, 2 * gates, beam_count), f32),
+            pltpu.VMEM((units, parts * 2 * BLOCK, width), f32),
+            pltpu.VMEM((units, parts + 2 * subs, 2 * BLOCK, width), f32),
+            pltpu.VMEM((subs, 2 * gates * BLOCK, local_channels), f32),
+            pltpu.VMEM((beam_count // 128, 2 * gates * BLOCK, 128), f32),
+            pltpu.VMEM((bins, 2 * gates, 2 * channels), bf16),
+            pltpu.VMEM((bins, 2 * gates, 2 * channels), bf16),
+            pltpu.VMEM((bins, 2 * gates, beam_count), bf16),
+            pltpu.VMEM((bins, 2 * gates, beam_count), bf16),
             pltpu.VMEM((bins, 1, beam_count), f32),
+            pltpu.VMEM((bins, gates, beam_count), f32),
             pltpu.VMEM((8, beam_count), f32),
             pltpu.VMEM((parts - 1, 8, beam_count), f32),
-            pltpu.SemaphoreType.DMA((INTERVALS, parts - 1)),
-            pltpu.SemaphoreType.DMA((INTERVALS, parts - 1)),
-            pltpu.SemaphoreType.DMA((INTERVALS,)),
+            pltpu.SemaphoreType.DMA((4,)),
+            pltpu.SemaphoreType.DMA,
+            pltpu.SemaphoreType.DMA((units, parts - 1)),
+            pltpu.SemaphoreType.DMA((units, parts - 1)),
+            pltpu.SemaphoreType.DMA((units,)),
             pltpu.SemaphoreType.DMA((parts - 1,)),
             pltpu.SemaphoreType.DMA((parts - 1,)),
+            pltpu.SemaphoreType.DMA((bins // BLOCK,)),
         ],
         compiler_params=pltpu.CompilerParams(
             collective_id=0, has_side_effects=True, vmem_limit_bytes=56 * 2**20
         ),
         name="beams",
-    )(flat, jnp.asarray(fourier_rows(parts)), taper, steer_real, steer_imag, range_taps, loading)
-    noise_level = jnp.sum(total, axis=0) / (PULSES * gates)
-    return (power / (noise_level + epsilon))[None]
+    )(
+        flat, jnp.asarray(fourier_rows(parts)), pulse_taper[None, :], channel_phase[None, :], beam_index[None, :],
+        range_taps, loading,
+    )
+    return (power / noise_level)[None]
 
 
 def solution(mesh):
@@ -444,8 +523,12 @@
         local_gates, local_channels = echoes.shape[2:]
         gates, channels = local_gates * sections, local_channels * subs
         fits = (
-            PULSES % parts == 0
-            and (PULSES // parts) % 8 == 0
+            parts & (parts - 1) == 0
+            and PULSES % parts == 0
+            and (PULSES // parts) % BLOCK == 0
+            and echoes.shape[1] == (INTERVALS - 1) * HOP + PULSES
+            and INTERVALS == 2
+            and ITERS == 2
             and gates % 8 == 0
             and 2 * gates <= channels
             and local_channels == 128

time: 84.4 us -> 65.5 us (0.78)
  Pallas kernels: 73.6 us -> 62.7 us
  other arithmetic: 7.21 us -> 1.9 us
  local copies, waits for them, and re-layouts: 2.68 us -> 0 us
    pallas_call x1, Pallas kernels: 73.6 us -> 62.7 us  [fused(): pl.pallas_call(functools.partial(kernel, sections, subs, gates, channels,...]
    unnamed x1 -> x0, local copies, waits for them, and re-layouts: 2.68 us -> none
    sin x1 -> x0, other arithmetic: 2.56 us -> none  [steering(): return (jnp.cos(phase_angle), jnp.sin(phase_angle))]
    concatenate x1 -> x0, other arithmetic: 1.35 us -> none  [fused(): taper = jnp.concatenate([pulse_taper, pulse_taper])[None, :]]
where the time goes in v1:
time: 65.5 us; the launch traced here: 65.3 us
  Pallas kernels  62.7 us (96%)
  other arithmetic  1.9 us (3%)
  between operations  0.66 us (1%)
    pallas_call x1, Pallas kernels, fused(): pl.pallas_call(functools.partial(kernel, sections, subs, gates, channels,...  62.7 us
    broadcast_in_dim x1, other arithmetic, fused(): return (power / noise_level)[None]  1.9 us

profile of v1, /device:TPU:0, one launch (start us, length us, event | category | flops | bytes accessed | tf_op | source)
XLA Modules:
  0.0 65.3 jit_solution(2441604939609090339)
XLA Ops:
  0.7 62.7 %beams.1 = (f32[16,32,256]{2,1,0:T(8,128)}, f32[1,256]{1,0:T(1,128)}) custom-call(f32[3072,128]{1,0:T(8,128)} %bitcast.7, f32[512,512]{1,0:T(8,128)} %constant.2.clone.rows_hbm, f32[1,256]{1,0:T(1,128)} %bitcast.8, f32[1,256]{1,0:T(1,128)} %bitcast.9, s32[1,256]{1,0:T(1,128)} %bitcast.10, f32[2,5]{1,0:T(2,128)} %taps_ref.1, f32[1]{0:T(128)S(6)} %copy.8.loading_ref), custom_call_target="tpu_custom_call" | custom-call | tf_op jit(solution)/shard_map/beams/pallas_call | solution.py:471
  63.4 1.9 %divide_bitcast_fusion = f32[1,16,32,256]{3,2,1,0:T(8,128)} fusion(f32[16,32,256]{2,1,0:T(8,128)} %get-tuple-element.7, f32[256]{0:T(256)} %bitcast.11), kind=kLoop, calls=%fused_computation | loop fusion | flops 131072 | bytes 1049600 | tf_op jit(solution)/shard_map/broadcast_in_dim | solution.py:515

commit v2 on v1

--- a/solution.py
+++ b/solution.py
@@ -423,7 +423,7 @@
     for group in range(groups_of_bins):
         refine(group, 1.0)
         lax.fori_loop(0, BLOCK, functools.partial(solve, group), 0, unroll=2)
-    total = jnp.zeros(sums.shape, f32)
+    total = jnp.zeros((8, sums.shape[1]), f32)
     out_copies = []
     for group in range(groups_of_bins):
         refine(groups_of_bins + group, -1.0)
@@ -432,6 +432,7 @@
         out_copies.append(pltpu.make_async_copy(power_ref.at[span], power_hbm.at[span], out_sem.at[group]))
         if group < groups_of_bins - 1:
             out_copies[-1].start()
+    total = jnp.sum(total, axis=0, keepdims=True)
     sums[...] = total
 
     def sum_piece(step):
@@ -451,7 +452,7 @@
         sum_piece(step).wait()
     for step in steps:
         total = total + gathered[step - 1]
-    noise_ref[...] = jnp.sum(total, axis=0, keepdims=True) / (PULSES * gates) + epsilon
+    noise_ref[...] = total / (PULSES * gates) + epsilon
     for copy in out_copies:
         copy.wait()
 
@@ -493,8 +494,8 @@
             pltpu.VMEM((bins, 2 * gates, beam_count), bf16),
             pltpu.VMEM((bins, 1, beam_count), f32),
             pltpu.VMEM((bins, gates, beam_count), f32),
-            pltpu.VMEM((8, beam_count), f32),
-            pltpu.VMEM((parts - 1, 8, beam_count), f32),
+            pltpu.VMEM((1, beam_count), f32),
+            pltpu.VMEM((parts - 1, 1, beam_count), f32),
             pltpu.SemaphoreType.DMA((4,)),
             pltpu.SemaphoreType.DMA,
             pltpu.SemaphoreType.DMA((units, parts - 1)),

time: 65.5 us -> 65.2 us (level)
  no operation moved by 1% of the time
where the time goes in v2:
time: 65.2 us; the launch traced here: 65 us
  Pallas kernels  62.5 us (96%)
  other arithmetic  1.9 us (3%)
  between operations  0.66 us (1%)
    pallas_call x1, Pallas kernels, fused(): pl.pallas_call(functools.partial(kernel, sections, subs, gates, channels,...  62.5 us
    broadcast_in_dim x1, other arithmetic, fused(): return (power / noise_level)[None]  1.9 us

profile of v2, /device:TPU:0, one launch (start us, length us, event | category | flops | bytes accessed | tf_op | source)
XLA Modules:
  0.0 65.0 jit_solution(2653148754484128834)
XLA Ops:
  0.7 62.5 %beams.1 = (f32[16,32,256]{2,1,0:T(8,128)}, f32[1,256]{1,0:T(1,128)}) custom-call(f32[3072,128]{1,0:T(8,128)} %bitcast.7, f32[512,512]{1,0:T(8,128)} %constant.2.clone.rows_hbm, f32[1,256]{1,0:T(1,128)} %bitcast.8, f32[1,256]{1,0:T(1,128)} %bitcast.9, s32[1,256]{1,0:T(1,128)} %bitcast.10, f32[2,5]{1,0:T(2,128)} %taps_ref.1, f32[1]{0:T(128)S(6)} %copy.8.loading_ref), custom_call_target="tpu_custom_call" | custom-call | tf_op jit(solution)/shard_map/beams/pallas_call | solution.py:472
  63.1 1.9 %divide_bitcast_fusion = f32[1,16,32,256]{3,2,1,0:T(8,128)} fusion(f32[16,32,256]{2,1,0:T(8,128)} %get-tuple-element.7, f32[256]{0:T(256)} %bitcast.11), kind=kLoop, calls=%fused_computation | loop fusion | flops 131072 | bytes 1049600 | tf_op jit(solution)/shard_map/broadcast_in_dim | solution.py:516
